TPU v7x, 256 devices: a whole 4x4x8 slice. The times are simulated.
256 devices in a mesh: sub: 64 (over x, z, core), blk: 4 (over y).
Axes of the slice: x: 4, y: 4, z: 8, core: 2. Of those that a mesh axis runs over, the one named last changes fastest.
Arguments:
- residual: float32 [64, 8, 375, 256], P('sub', 'blk'), may hold values from -6 to 6
- stiffness: bfloat16 [64, 8, 16, 375, 375], P('sub', 'blk'), may hold values from -0.078125 to 0.078125
- pattern: int32 [64, 8, 16], P('sub', 'blk'), may hold values from 0 to 7
- neumann_inv: bfloat16 [64, 8, 375, 375], P('sub', 'blk'), may hold values from -0.3125 to 0.3125
- dirichlet_inv: bfloat16 [64, 8, 375, 375], P('sub', 'blk'), may hold values from -0.3125 to 0.3125
- basis: bfloat16 [64, 8, 375, 192], P('sub', 'blk'), may hold values from -0.5 to 0.5
- node_ops: float32 [64, 6, 192, 192], P('sub'), as said below
- root_inv: float32 [192, 192], replicated, may hold values from -0.4375 to 0.4375
Outputs:
- preconditioned: float32 [64, 8, 375, 256], P('sub', 'blk')
Inputs may be any that keep to these rules, and one draw needn't show every extreme that they name: node_ops[s, l] equals node_ops[t, l] whenever s // 2**l == t // 2**l: one map for each tree node, held by all of its subdomains.
All inputs are finite; a program needn't handle non-finite values.
Results may differ from a plain program's by a relative error of at most 0.004.
Values may be sent and summed in bfloat16 or wider, within the bound.
A program may use at most 64 MiB of HBM per device.

v0:
```python
import jax
import jax.numpy as jnp
from jax import lax
from jax.sharding import PartitionSpec as P


def swapped(x, axis, distance):
    return lax.ppermute(x, axis, [(i, i ^ 1 << distance) for i in range(lax.axis_size(axis))])


def passed_along(x, axis, by):
    count = lax.axis_size(axis)
    pairs = [(i, i + by) for i in range(count) if 0 <= i + by < count]
    return lax.ppermute(x, axis, pairs)


def tree_solve(values, maps, root_inv):
    highest = lax.Precision.HIGHEST
    level_values = [values]
    current = values
    for level in range(maps.shape[0]):
        own = jnp.einsum("mk,mr->kr", maps[level], current, precision=highest)
        current = own + swapped(own, "sub", level)
        level_values.append(current)
    field = jnp.dot(root_inv, current, precision=highest)
    for level in reversed(range(maps.shape[0])):
        field = jnp.dot(maps[level], field, precision=highest) + level_values[level]
    return field


def shards(residual, stiffness, pattern, neumann_inv, dirichlet_inv, basis, node_ops, root_inv):
    subs = lax.axis_size("sub")
    here = lax.axis_index("sub")
    per_device = residual.shape[1]
    local_ids = jnp.arange(per_device)
    shared = (local_ids == 0) & (here > 0) | (local_ids == per_device - 1) & (here < subs - 1)
    scale = jnp.where(shared, 0.5, 1.0).astype(jnp.float32)[:, None, None]
    scaled_bf = (residual[0] * scale).astype(jnp.bfloat16)
    local_fix = jnp.einsum(
        "jab,jbr->jar", neumann_inv[0], scaled_bf, preferred_element_type=jnp.float32
    )
    partial_coarse = jnp.einsum(
        "jbm,jbr->mr", basis[0], scaled_bf, preferred_element_type=jnp.float32
    )
    total = lax.psum(partial_coarse, "blk")
    coarse_fix = tree_solve(total, node_ops[0], root_inv).astype(jnp.bfloat16)
    fix_term = jnp.einsum("jbm,mr->jbr", basis[0], coarse_fix, preferred_element_type=jnp.float32)
    combined = ((local_fix + fix_term) * scale)[None]
    incoming = passed_along(combined[:, -1], "sub", 1)
    first = combined[:, 0] + incoming
    returned = passed_along(first, "sub", -1)
    last = jnp.where(here < subs - 1, returned, combined[:, -1])
    assembled = jnp.concatenate([first[:, None], combined[:, 1:-1], last[:, None]], axis=1)
    assembled_bf = assembled.astype(jnp.bfloat16)
    gathered = lax.all_gather(assembled_bf, "blk", axis=1, tiled=True)
    picked = jnp.take(gathered[0], pattern[0], axis=0)
    coupled = jnp.einsum("jpab,jpbr->jar", stiffness[0], picked, preferred_element_type=jnp.float32)
    correction = jnp.einsum(
        "jab,jbr->jar",
        dirichlet_inv[0],
        coupled.astype(jnp.bfloat16),
        preferred_element_type=jnp.float32,
    )
    result = assembled[0] - jnp.where(shared[:, None, None], 0.0, correction)
    return result[None]


def solution(mesh):
    placed = (
        P("sub", "blk", None, None),
        P("sub", "blk", None, None, None),
        P("sub", "blk", None),
        P("sub", "blk", None, None),
        P("sub", "blk", None, None),
        P("sub", "blk", None, None),
        P("sub", None, None, None),
        P(),
    )
    return jax.shard_map(
        shards, mesh=mesh, in_specs=placed, out_specs=P("sub", "blk", None, None), check_vma=False
    )
```

profile of v0, /device:TPU:1, one launch (start us, length us, event | category | flops | bytes accessed | tf_op | source)
XLA Modules:
  0.0 188.2 jit_solution(13424925944676565091)
XLA Ops:
  6.5 0.0 copy-start
  6.5 0.0 copy-start.1
  6.5 0.0 all-reduce.2.cloned.1.call-start
  6.6 2.3 %convolution_bitcast_fusion.14 = f32[192,256]{1,0:T(8,128)} fusion(bf16[1,2,375,192]{2,3,1,0:T(8,128)(2,1)} %param.13, f32[1,2,375,256]{3,1,2,0:T(2,128)} %param.8, f32[2]{0:T(128)S(1)} %get-tuple-element.5), kind=kOutput, calls=%fused_computation.31 | convolution fusion | flops 74112000 | bytes 1252616 | tf_op jit(solution)/shard_map/jbm,jbr->mr/dot_general | solution.py:42
  8.9 0.0 all-reduce.2.cloned.1.call-update
  8.9 0.0 all-gather.2.cloned.1.call-start
  8.9 49.2 %all-reduce.2.cloned.1.call-done = f32[192,256]{1,0:T(8,128)} async-done(((f32[192,256]{1,0:T(8,128)}), f32[192,256]{1,0:T(8,128)}) %all-reduce.2.cloned.1.call-update) | async-done | bytes 196624 | tf_op jit(solution)/shard_map/psum | solution.py:45
  58.2 0.0 copy-done.1
  58.2 1.5 convolution_bitcast_fusion.13
  59.7 2.9 %collective-permute-start = (f32[192,256]{1,0:T(8,128)S(1)}, f32[192,256]{1,0:T(8,128)S(1)}, u32[]{:S(2)}, u32[]{:S(2)}) collective-permute-start(f32[192,256]{1,0:T(8,128)S(1)} %convolution_bitcast_fusion.13), channel_id=1, source_target_pairs={{0,4},{4,0},{8,12},{12,8},{16,20},{20,16},{24,28},{28,24},{32,36},... | collective-permute-start | bytes 589832 | tf_op jit(solution)/shard_map/ppermute | solution.py:8
  62.6 1.1 collective-permute-done
  63.6 0.6 convolution_bitcast_fusion.12
  64.2 1.4 collective-permute-start.1
  65.6 4.8 %collective-permute-done.1 = f32[192,256]{1,0:T(8,128)S(1)} collective-permute-done((f32[192,256]{1,0:T(8,128)S(1)}, f32[192,256]{1,0:T(8,128)S(1)}, u32[]{:S(2)}, u32[]{:S(2)}) %collective-permute-start.1) | collective-permute-done | bytes 196640 | tf_op jit(solution)/shard_map/ppermute | solution.py:8
  70.4 0.6 convolution_bitcast_fusion.11
  71.0 2.3 %collective-permute-start.2 = (f32[192,256]{1,0:T(8,128)S(1)}, f32[192,256]{1,0:T(8,128)S(1)}, u32[]{:S(2)}, u32[]{:S(2)}) collective-permute-start(f32[192,256]{1,0:T(8,128)S(1)} %convolution_bitcast_fusion.11), channel_id=1, source_target_pairs={{0,16},{4,20},{8,24},{12,28},{16,0},{20,4},{24,8},{28,12},{32,48},... | collective-permute-start | bytes 589832 | tf_op jit(solution)/shard_map/ppermute | solution.py:8
  73.4 8.7 %collective-permute-done.2 = f32[192,256]{1,0:T(8,128)S(1)} collective-permute-done((f32[192,256]{1,0:T(8,128)S(1)}, f32[192,256]{1,0:T(8,128)S(1)}, u32[]{:S(2)}, u32[]{:S(2)}) %collective-permute-start.2) | collective-permute-done | bytes 196640 | tf_op jit(solution)/shard_map/ppermute | solution.py:8
  82.1 0.6 convolution_bitcast_fusion.10
  82.7 0.0 copy-start.5
  82.7 6.4 %collective-permute-start.3 = (f32[192,256]{1,0:T(8,128)S(1)}, f32[192,256]{1,0:T(8,128)S(1)}, u32[]{:S(2)}, u32[]{:S(2)}) collective-permute-start(f32[192,256]{1,0:T(8,128)S(1)} %convolution_bitcast_fusion.10), channel_id=1, source_target_pairs={{0,32},{4,36},{8,40},{12,44},{16,48},{20,52},{24,56},{28,60},{32,0... | collective-permute-start | bytes 589832 | tf_op jit(solution)/shard_map/ppermute | solution.py:8
  89.1 7.4 %collective-permute-done.3 = f32[192,256]{1,0:T(8,128)S(1)} collective-permute-done((f32[192,256]{1,0:T(8,128)S(1)}, f32[192,256]{1,0:T(8,128)S(1)}, u32[]{:S(2)}, u32[]{:S(2)}) %collective-permute-start.3) | collective-permute-done | bytes 196640 | tf_op jit(solution)/shard_map/ppermute | solution.py:8
  96.6 0.6 convolution_bitcast_fusion.9
  97.2 1.3 collective-permute-start.4
  98.4 3.9 %collective-permute-done.4 = f32[192,256]{1,0:T(8,128)S(1)} collective-permute-done((f32[192,256]{1,0:T(8,128)S(1)}, f32[192,256]{1,0:T(8,128)S(1)}, u32[]{:S(2)}, u32[]{:S(2)}) %collective-permute-start.4) | collective-permute-done | bytes 196640 | tf_op jit(solution)/shard_map/ppermute | solution.py:8
  102.3 0.6 convolution_bitcast_fusion.8
  102.9 2.8 %collective-permute-start.5 = (f32[192,256]{1,0:T(8,128)S(1)}, f32[192,256]{1,0:T(8,128)S(1)}, u32[]{:S(2)}, u32[]{:S(2)}) collective-permute-start(f32[192,256]{1,0:T(8,128)S(1)} %convolution_bitcast_fusion.8), channel_id=1, source_target_pairs={{0,128},{4,132},{8,136},{12,140},{16,144},{20,148},{24,152},{28,15... | collective-permute-start | bytes 589832 | tf_op jit(solution)/shard_map/ppermute | solution.py:8
  105.7 3.3 %collective-permute-done.5 = f32[192,256]{1,0:T(8,128)S(1)} collective-permute-done((f32[192,256]{1,0:T(8,128)S(1)}, f32[192,256]{1,0:T(8,128)S(1)}, u32[]{:S(2)}, u32[]{:S(2)}) %collective-permute-start.5) | collective-permute-done | bytes 196640 | tf_op jit(solution)/shard_map/ppermute | solution.py:8
  109.0 0.0 copy-done.5
  109.0 0.3 fusion.52
  109.4 0.3 fusion.23
  109.7 0.3 fusion.22
  110.0 0.0 copy-start.4
  110.0 0.3 fusion.21
  110.4 0.0 copy-start.3
  110.4 0.3 fusion.20
  110.7 0.0 copy-start.2
  110.7 0.3 fusion.19
  111.1 0.0 copy-done.4
  111.1 0.3 fusion.25
  111.4 0.0 copy-done.3
  111.4 0.3 convolution_bitcast_fusion.1
  111.8 0.0 copy-done
  111.8 0.1 copy-done.2
  111.9 0.4 fusion.12
  112.3 0.1 fusion.70
  112.4 0.4 copy.61
  112.8 2.7 %collective-permute-start.6 = (f32[1,375,256]{2,0,1:T(1,128)S(1)}, f32[1,375,256]{2,0,1:T(1,128)S(1)}, u32[]{:S(2)}, u32[]{:S(2)}) collective-permute-start(f32[1,375,256]{2,0,1:T(1,128)S(1)} %bitcast.158), channel_id=1, source_target_pairs={{0,4},{4,8},{8,12},{12,16},{16,20},{20,24},{24,28},{28,32},{32,36}... | collective-permute-start | bytes 1152008 | tf_op jit(solution)/shard_map/ppermute | solution.py:14
  115.5 4.6 %collective-permute-done.6 = f32[1,375,256]{2,0,1:T(1,128)S(1)} collective-permute-done((f32[1,375,256]{2,0,1:T(1,128)S(1)}, f32[1,375,256]{2,0,1:T(1,128)S(1)}, u32[]{:S(2)}, u32[]{:S(2)}) %collective-permute-start.6) | collective-permute-done | bytes 384032 | tf_op jit(solution)/shard_map/ppermute | solution.py:14
  120.1 0.5 fusion.36
  120.6 2.1 %collective-permute-start.7 = (f32[1,375,256]{2,0,1:T(1,128)S(1)}, f32[1,375,256]{2,0,1:T(1,128)S(1)}, u32[]{:S(2)}, u32[]{:S(2)}) collective-permute-start(f32[1,375,256]{2,0,1:T(1,128)S(1)} %fusion.36), channel_id=1, source_target_pairs={{4,0},{8,4},{12,8},{16,12},{20,16},{24,20},{28,24},{32,28},{36,32}... | collective-permute-start | bytes 1152008 | tf_op jit(solution)/shard_map/ppermute | solution.py:14
  122.7 7.6 %collective-permute-done.7 = f32[1,375,256]{2,0,1:T(1,128)S(1)} collective-permute-done((f32[1,375,256]{2,0,1:T(1,128)S(1)}, f32[1,375,256]{2,0,1:T(1,128)S(1)}, u32[]{:S(2)}, u32[]{:S(2)}) %collective-permute-start.7) | collective-permute-done | bytes 384032 | tf_op jit(solution)/shard_map/ppermute | solution.py:14
  130.3 0.5 fusion.35
  130.8 0.0 copy-start.6
  130.8 0.7 fusion.39
  131.6 0.8 copy.30
  132.3 0.0 all-gather.2.cloned.1.call-update
  132.4 0.0 copy-done.6
  132.4 0.1 reshape.96
  132.5 31.0 %all-gather.2.cloned.1.call-done = bf16[1,8,375,256]{3,2,0,1:T(8,128)(2,1)} async-done(((bf16[1,2,375,256]{3,2,0,1:T(8,128)(2,1)}), bf16[1,8,375,256]{3,2,0,1:T(8,128)(2,1)}) %all-gather.2.cloned.1.call-update) | async-done | bytes 1536016 | tf_op jit(solution)/shard_map/all_gather | solution.py:55
  163.5 0.0 copy-start.7
  163.5 5.0 %gather_fusion = bf16[32,375,256]{2,1,0:T(8,128)(2,1)} fusion(bf16[8,375,256]{2,1,0:T(8,128)(2,1)} %bitcast.154, s32[1024]{0:T(1024)S(1)} %pad_clamp_fusion), kind=kCustom, calls=%fused_computation | custom fusion | bytes 12288128 | tf_op jit(solution)/shard_map/jit(_take)/gather | solution.py:56
  168.5 0.0 copy-done.7
  168.5 11.0 %fusion.28 = f32[2,256,375]{1,2,0:T(8,128)S(1)} fusion(bf16[2,375,375]{2,0,1:T(2,128)(2,1)S(1)} %bitcast.160, bf16[2,16,375,375]{3,1,2,0:T(8,128)(2,1)} %bitcast.159, bf16[2,16,375,256]{3,2,1,0:T(8,128)(2,1)} %bitcast.155, pred[2,16]{1,0:T(4,128)(4,1)S(1)} %compare_and_fusion), kind=kOutput, calls=%fused_computation.41 | convolution fusion | flops 2451264000 | bytes 16474532 | tf_op jit(solution)/shard_map/jab,jbr->jar/dot_general | solution.py:58
  179.6 1.8 fusion.27
  (9 shorter events, 0.2 us)
Async XLA Ops:
  6.5 105.2 %copy-start = (bf16[1,2,375,375]{3,1,2,0:T(2,128)(2,1)S(1)}, bf16[1,2,375,375]{3,1,2,0:T(2,128)(2,1)}, u32[]{:S(2)}) copy-start(bf16[1,2,375,375]{3,1,2,0:T(2,128)(2,1)} %param.11) | copy-start | bytes 1687504
  6.5 51.6 %copy-start.1 = (f32[1,6,192,192]{3,2,1,0:T(8,128)S(1)}, f32[1,6,192,192]{3,2,1,0:T(8,128)}, u32[]{:S(2)}) copy-start(f32[1,6,192,192]{3,2,1,0:T(8,128)} %param.14) | copy-start | bytes 2654212
  6.5 51.6 %all-reduce.2.cloned.1.call-start = ((), (), s32[]{:S(2)}) async-start(), calls=%async_computation | async-start | bytes 393216 | tf_op jit(solution)/shard_map/psum | solution.py:45
  8.9 154.6 %all-gather.2.cloned.1.call-start = ((), (), s32[]{:S(2)}) async-start(), calls=%async_computation.1 | async-start | bytes 1925120 | tf_op jit(solution)/shard_map/all_gather | solution.py:55
  59.7 3.9 %collective-permute-start = (f32[192,256]{1,0:T(8,128)S(1)}, f32[192,256]{1,0:T(8,128)S(1)}, u32[]{:S(2)}, u32[]{:S(2)}) collective-permute-start(f32[192,256]{1,0:T(8,128)S(1)} %convolution_bitcast_fusion.13), channel_id=1, source_target_pairs={{0,4},{4,0},{8,12},{12,8},{16,20},{20,16},{24,28},{28,24},{32,36},... | collective-permute-start | bytes 589832 | tf_op jit(solution)/shard_map/ppermute | solution.py:8
  64.2 6.2 %collective-permute-start.1 = (f32[192,256]{1,0:T(8,128)S(1)}, f32[192,256]{1,0:T(8,128)S(1)}, u32[]{:S(2)}, u32[]{:S(2)}) collective-permute-start(f32[192,256]{1,0:T(8,128)S(1)} %convolution_bitcast_fusion.12), channel_id=1, source_target_pairs={{0,8},{4,12},{8,0},{12,4},{16,24},{20,28},{24,16},{28,20},{32,40},... | collective-permute-start | bytes 589832 | tf_op jit(solution)/shard_map/ppermute | solution.py:8
  71.0 11.0 %collective-permute-start.2 = (f32[192,256]{1,0:T(8,128)S(1)}, f32[192,256]{1,0:T(8,128)S(1)}, u32[]{:S(2)}, u32[]{:S(2)}) collective-permute-start(f32[192,256]{1,0:T(8,128)S(1)} %convolution_bitcast_fusion.11), channel_id=1, source_target_pairs={{0,16},{4,20},{8,24},{12,28},{16,0},{20,4},{24,8},{28,12},{32,48},... | collective-permute-start | bytes 589832 | tf_op jit(solution)/shard_map/ppermute | solution.py:8
  82.7 26.4 %copy-start.5 = (f32[192,192]{1,0:T(8,128)S(1)}, f32[192,192]{1,0:T(8,128)}, u32[]{:S(2)}) copy-start(f32[192,192]{1,0:T(8,128)} %param.15) | copy-start | bytes 442372
  82.7 13.9 %collective-permute-start.3 = (f32[192,256]{1,0:T(8,128)S(1)}, f32[192,256]{1,0:T(8,128)S(1)}, u32[]{:S(2)}, u32[]{:S(2)}) collective-permute-start(f32[192,256]{1,0:T(8,128)S(1)} %convolution_bitcast_fusion.10), channel_id=1, source_target_pairs={{0,32},{4,36},{8,40},{12,44},{16,48},{20,52},{24,56},{28,60},{32,0... | collective-permute-start | bytes 589832 | tf_op jit(solution)/shard_map/ppermute | solution.py:8
  97.2 5.1 %collective-permute-start.4 = (f32[192,256]{1,0:T(8,128)S(1)}, f32[192,256]{1,0:T(8,128)S(1)}, u32[]{:S(2)}, u32[]{:S(2)}) collective-permute-start(f32[192,256]{1,0:T(8,128)S(1)} %convolution_bitcast_fusion.9), channel_id=1, source_target_pairs={{0,64},{4,68},{8,72},{12,76},{16,80},{20,84},{24,88},{28,92},{32,9... | collective-permute-start | bytes 589832 | tf_op jit(solution)/shard_map/ppermute | solution.py:8
  102.9 6.1 %collective-permute-start.5 = (f32[192,256]{1,0:T(8,128)S(1)}, f32[192,256]{1,0:T(8,128)S(1)}, u32[]{:S(2)}, u32[]{:S(2)}) collective-permute-start(f32[192,256]{1,0:T(8,128)S(1)} %convolution_bitcast_fusion.8), channel_id=1, source_target_pairs={{0,128},{4,132},{8,136},{12,140},{16,144},{20,148},{24,152},{28,15... | collective-permute-start | bytes 589832 | tf_op jit(solution)/shard_map/ppermute | solution.py:8
  110.0 1.0 copy-start.4
  110.4 1.0 copy-start.3
  110.7 1.1 copy-start.2
  112.8 7.3 %collective-permute-start.6 = (f32[1,375,256]{2,0,1:T(1,128)S(1)}, f32[1,375,256]{2,0,1:T(1,128)S(1)}, u32[]{:S(2)}, u32[]{:S(2)}) collective-permute-start(f32[1,375,256]{2,0,1:T(1,128)S(1)} %bitcast.158), channel_id=1, source_target_pairs={{0,4},{4,8},{8,12},{12,16},{16,20},{20,24},{24,28},{28,32},{32,36}... | collective-permute-start | bytes 1152008 | tf_op jit(solution)/shard_map/ppermute | solution.py:14
  120.6 9.7 %collective-permute-start.7 = (f32[1,375,256]{2,0,1:T(1,128)S(1)}, f32[1,375,256]{2,0,1:T(1,128)S(1)}, u32[]{:S(2)}, u32[]{:S(2)}) collective-permute-start(f32[1,375,256]{2,0,1:T(1,128)S(1)} %fusion.36), channel_id=1, source_target_pairs={{4,0},{8,4},{12,8},{16,12},{20,16},{24,20},{28,24},{32,28},{36,32}... | collective-permute-start | bytes 1152008 | tf_op jit(solution)/shard_map/ppermute | solution.py:14
  130.8 1.5 copy-start.6
  163.5 5.0 %copy-start.7 = (bf16[1,2,375,375]{3,1,2,0:T(2,128)(2,1)S(1)}, bf16[1,2,375,375]{3,1,2,0:T(2,128)(2,1)}, u32[]{:S(2)}) copy-start(bf16[1,2,375,375]{3,1,2,0:T(2,128)(2,1)} %param.12) | copy-start | bytes 1687504
Sparse Core Ops, SparseCore 0:
  9.7 48.4 all-reduce.1
  132.5 30.9 all-gather.1
where the time goes:
time: 188 us
  waiting for transfers between devices  122 us (65%)
  starting transfers between devices  21.9 us (12%)
  matrix products  20.8 us (11%)
  between operations  13.6 us (7%)
  local copies, waits for them, and re-layouts  6.44 us (3%)
  other arithmetic  3.71 us (2%)
    psum x1, waiting for transfers between devices, shards(): total = lax.psum(partial_coarse, 'blk')  49.2 us
    all_gather x1, waiting for transfers between devices, shards(): gathered = lax.all_gather(assembled_bf, 'blk', axis=1, tiled=True)  31 us
    ppermute x6, waiting for transfers between devices, swapped(): lax.ppermute(x, axis, [(i, i ^ 1 << distance) for i in range(lax.axis_siz...  29.2 us
    ppermute x6, starting transfers between devices, swapped(): lax.ppermute(x, axis, [(i, i ^ 1 << distance) for i in range(lax.axis_siz...  17.1 us
    ppermute x2, waiting for transfers between devices, passed_along(): return lax.ppermute(x, axis, pairs)  12.2 us
    dot_general x1, matrix products, shards(): jnp.einsum('jab,jbr->jar', dirichlet_inv[0], coupled.astype(jnp.bfloat16)...  11 us
    gather x1, local copies, waits for them, and re-layouts, shards(): picked = jnp.take(gathered[0], pattern[0], axis=0)  5.01 us
    ppermute x2, starting transfers between devices, passed_along(): return lax.ppermute(x, axis, pairs)  4.79 us
  transfers between devices with their start and end apart: 10, of which 10 were waited for; matrix products, arithmetic and copies ran while one was open for 0% of the time, Pallas kernels for 0%

commit v1 on v0

--- a/solution.py
+++ b/solution.py
@@ -42,7 +42,9 @@
     partial_coarse = jnp.einsum(
         "jbm,jbr->mr", basis[0], scaled_bf, preferred_element_type=jnp.float32
     )
-    total = lax.psum(partial_coarse, "blk")
+    total = partial_coarse
+    for hop in (1, 2):
+        total = total + lax.ppermute(total, "blk", [(dev, dev ^ hop) for dev in range(4)])
     coarse_fix = tree_solve(total, node_ops[0], root_inv).astype(jnp.bfloat16)
     fix_term = jnp.einsum("jbm,mr->jbr", basis[0], coarse_fix, preferred_element_type=jnp.float32)
     combined = ((local_fix + fix_term) * scale)[None]

time: 188 us -> 159 us (0.85)
  waiting for transfers between devices: 122 us -> 79.6 us
  starting transfers between devices: 21.9 us -> 30.3 us
  matrix products: 20.8 us -> 24.8 us
    psum x1 -> x0, waiting for transfers between devices: 49.2 us -> none  [shards(): total = lax.psum(partial_coarse, 'blk')]
    ppermute x0 -> x2, waiting for transfers between devices: none -> 6.51 us  [shards(): lax.ppermute(total, 'blk', [(dev, dev ^ hop) for dev in range(4)])]
    ppermute x0 -> x2, starting transfers between devices: none -> 6.24 us  [shards(): lax.ppermute(total, 'blk', [(dev, dev ^ hop) for dev in range(4)])]
    dot_general x6, matrix products: 4.43 us -> 9.17 us  [tree_solve(): own = jnp.einsum('mk,mr->kr', maps[level], current, precision=highest)]
  transfers between devices with their start and end apart: 10 -> 11, of which waited for: 10 -> 11; matrix products, arithmetic and copies ran while one was open for 0% -> 0% of each run, Pallas kernels for 0% -> 0%
where the time goes in v1:
time: 159 us
  waiting for transfers between devices  79.6 us (50%)
  starting transfers between devices  30.3 us (19%)
  matrix products  24.8 us (16%)
  between operations  13.6 us (9%)
  local copies, waits for them, and re-layouts  6.46 us (4%)
  other arithmetic  3.76 us (2%)
    all_gather x1, waiting for transfers between devices, shards(): gathered = lax.all_gather(assembled_bf, 'blk', axis=1, tiled=True)  32 us
    ppermute x6, waiting for transfers between devices, swapped(): lax.ppermute(x, axis, [(i, i ^ 1 << distance) for i in range(lax.axis_siz...  28.9 us
    ppermute x6, starting transfers between devices, swapped(): lax.ppermute(x, axis, [(i, i ^ 1 << distance) for i in range(lax.axis_siz...  18.2 us
    ppermute x2, waiting for transfers between devices, passed_along(): return lax.ppermute(x, axis, pairs)  12.2 us
    dot_general x1, matrix products, shards(): jnp.einsum('jab,jbr->jar', dirichlet_inv[0], coupled.astype(jnp.bfloat16)...  11 us
    dot_general x6, matrix products, tree_solve(): own = jnp.einsum('mk,mr->kr', maps[level], current, precision=highest)  9.17 us
    ppermute x2, waiting for transfers between devices, shards(): lax.ppermute(total, 'blk', [(dev, dev ^ hop) for dev in range(4)])  6.51 us
    ppermute x2, starting transfers between devices, shards(): lax.ppermute(total, 'blk', [(dev, dev ^ hop) for dev in range(4)])  6.24 us
  transfers between devices with their start and end apart: 11, of which 11 were waited for; matrix products, arithmetic and copies ran while one was open for 0% of the time, Pallas kernels for 0%

profile of v1, /device:TPU:1, one launch (start us, length us, event | category | flops | bytes accessed | tf_op | source)
XLA Modules:
  0.0 158.7 jit_solution(10859131019039054373)
XLA Ops:
  6.5 0.0 copy-start
  6.5 0.0 all-gather.2.cloned.1.call-start
  6.5 1.6 convolution_bitcast_fusion.14
  8.1 2.2 %collective-permute-start = (f32[192,256]{1,0:T(8,128)S(1)}, f32[192,256]{1,0:T(8,128)S(1)}, u32[]{:S(2)}, u32[]{:S(2)}) collective-permute-start(f32[192,256]{1,0:T(8,128)S(1)} %convolution_bitcast_fusion.14), channel_id=1, source_target_pairs={{0,1},{1,0},{2,3},{3,2},{4,5},{5,4},{6,7},{7,6},{8,9},{9,8},{10,11... | collective-permute-start | bytes 589832 | tf_op jit(solution)/shard_map/ppermute | solution.py:47
  10.3 3.4 %collective-permute-done = f32[192,256]{1,0:T(8,128)S(1)} collective-permute-done((f32[192,256]{1,0:T(8,128)S(1)}, f32[192,256]{1,0:T(8,128)S(1)}, u32[]{:S(2)}, u32[]{:S(2)}) %collective-permute-start) | collective-permute-done | bytes 196640 | tf_op jit(solution)/shard_map/ppermute | solution.py:47
  13.8 4.0 %collective-permute-start.1 = (f32[192,256]{1,0:T(8,128)S(1)}, f32[192,256]{1,0:T(8,128)S(1)}, u32[]{:S(2)}, u32[]{:S(2)}) collective-permute-start(f32[192,256]{1,0:T(8,128)S(1)} %add.69), channel_id=1, source_target_pairs={{0,2},{1,3},{2,0},{3,1},{4,6},{5,7},{6,4},{7,5},{8,10},{9,11},{10,... | collective-permute-start | bytes 589832 | tf_op jit(solution)/shard_map/ppermute | solution.py:47
  17.8 3.1 %collective-permute-done.1 = f32[192,256]{1,0:T(8,128)S(1)} collective-permute-done((f32[192,256]{1,0:T(8,128)S(1)}, f32[192,256]{1,0:T(8,128)S(1)}, u32[]{:S(2)}, u32[]{:S(2)}) %collective-permute-start.1) | collective-permute-done | bytes 196640 | tf_op jit(solution)/shard_map/ppermute | solution.py:47
  20.9 1.5 convolution_bitcast_fusion.13
  22.4 3.6 %collective-permute-start.2 = (f32[192,256]{1,0:T(8,128)S(1)}, f32[192,256]{1,0:T(8,128)S(1)}, u32[]{:S(2)}, u32[]{:S(2)}) collective-permute-start(f32[192,256]{1,0:T(8,128)S(1)} %convolution_bitcast_fusion.13), channel_id=1, source_target_pairs={{0,4},{4,0},{8,12},{12,8},{16,20},{20,16},{24,28},{28,24},{32,36},... | collective-permute-start | bytes 589832 | tf_op jit(solution)/shard_map/ppermute | solution.py:8
  26.0 1.1 collective-permute-done.2
  27.1 1.5 convolution_bitcast_fusion.12
  28.6 1.1 collective-permute-start.3
  29.7 5.1 %collective-permute-done.3 = f32[192,256]{1,0:T(8,128)S(1)} collective-permute-done((f32[192,256]{1,0:T(8,128)S(1)}, f32[192,256]{1,0:T(8,128)S(1)}, u32[]{:S(2)}, u32[]{:S(2)}) %collective-permute-start.3) | collective-permute-done | bytes 196640 | tf_op jit(solution)/shard_map/ppermute | solution.py:8
  34.8 1.5 convolution_bitcast_fusion.11
  36.3 2.8 %collective-permute-start.4 = (f32[192,256]{1,0:T(8,128)S(1)}, f32[192,256]{1,0:T(8,128)S(1)}, u32[]{:S(2)}, u32[]{:S(2)}) collective-permute-start(f32[192,256]{1,0:T(8,128)S(1)} %convolution_bitcast_fusion.11), channel_id=1, source_target_pairs={{0,16},{4,20},{8,24},{12,28},{16,0},{20,4},{24,8},{28,12},{32,48},... | collective-permute-start | bytes 589832 | tf_op jit(solution)/shard_map/ppermute | solution.py:8
  39.1 8.6 %collective-permute-done.4 = f32[192,256]{1,0:T(8,128)S(1)} collective-permute-done((f32[192,256]{1,0:T(8,128)S(1)}, f32[192,256]{1,0:T(8,128)S(1)}, u32[]{:S(2)}, u32[]{:S(2)}) %collective-permute-start.4) | collective-permute-done | bytes 196640 | tf_op jit(solution)/shard_map/ppermute | solution.py:8
  47.7 1.5 convolution_bitcast_fusion.10
  49.3 0.0 copy-start.4
  49.3 6.5 %collective-permute-start.5 = (f32[192,256]{1,0:T(8,128)S(1)}, f32[192,256]{1,0:T(8,128)S(1)}, u32[]{:S(2)}, u32[]{:S(2)}) collective-permute-start(f32[192,256]{1,0:T(8,128)S(1)} %convolution_bitcast_fusion.10), channel_id=1, source_target_pairs={{0,32},{4,36},{8,40},{12,44},{16,48},{20,52},{24,56},{28,60},{32,0... | collective-permute-start | bytes 589832 | tf_op jit(solution)/shard_map/ppermute | solution.py:8
  55.8 7.2 %collective-permute-done.5 = f32[192,256]{1,0:T(8,128)S(1)} collective-permute-done((f32[192,256]{1,0:T(8,128)S(1)}, f32[192,256]{1,0:T(8,128)S(1)}, u32[]{:S(2)}, u32[]{:S(2)}) %collective-permute-start.5) | collective-permute-done | bytes 196640 | tf_op jit(solution)/shard_map/ppermute | solution.py:8
  63.1 0.0 copy-start.1
  63.1 1.6 %convolution_bitcast_fusion.9 = f32[192,256]{1,0:T(8,128)S(1)} fusion(f32[192,256]{1,0:T(8,128)S(1)} %add.74, f32[1,6,192,192]{3,2,1,0:T(8,128)} %param.14), kind=kOutput, calls=%fused_computation.26 | convolution fusion | flops 113246208 | bytes 589824 | tf_op jit(solution)/shard_map/mk,mr->kr/dot_general | solution.py:22
  64.7 1.3 collective-permute-start.6
  66.0 3.6 %collective-permute-done.6 = f32[192,256]{1,0:T(8,128)S(1)} collective-permute-done((f32[192,256]{1,0:T(8,128)S(1)}, f32[192,256]{1,0:T(8,128)S(1)}, u32[]{:S(2)}, u32[]{:S(2)}) %collective-permute-start.6) | collective-permute-done | bytes 196640 | tf_op jit(solution)/shard_map/ppermute | solution.py:8
  69.7 1.5 convolution_bitcast_fusion.8
  71.2 2.8 %collective-permute-start.7 = (f32[192,256]{1,0:T(8,128)S(1)}, f32[192,256]{1,0:T(8,128)S(1)}, u32[]{:S(2)}, u32[]{:S(2)}) collective-permute-start(f32[192,256]{1,0:T(8,128)S(1)} %convolution_bitcast_fusion.8), channel_id=1, source_target_pairs={{0,128},{4,132},{8,136},{12,140},{16,144},{20,148},{24,152},{28,15... | collective-permute-start | bytes 589832 | tf_op jit(solution)/shard_map/ppermute | solution.py:8
  74.0 3.3 %collective-permute-done.7 = f32[192,256]{1,0:T(8,128)S(1)} collective-permute-done((f32[192,256]{1,0:T(8,128)S(1)}, f32[192,256]{1,0:T(8,128)S(1)}, u32[]{:S(2)}, u32[]{:S(2)}) %collective-permute-start.7) | collective-permute-done | bytes 196640 | tf_op jit(solution)/shard_map/ppermute | solution.py:8
  77.3 0.0 copy-done.4
  77.3 0.3 fusion.52
  77.7 0.0 copy-done.1
  77.7 0.3 fusion.23
  78.0 0.3 fusion.22
  78.4 0.3 fusion.21
  78.7 0.0 copy-start.3
  78.7 0.3 fusion.20
  79.0 0.0 copy-start.2
  79.1 0.3 fusion.19
  79.4 0.3 fusion.25
  79.7 0.0 copy-done.3
  79.7 0.3 convolution_bitcast_fusion.1
  80.1 0.0 copy-done
  80.1 0.1 copy-done.2
  80.2 0.4 fusion.12
  80.6 0.1 fusion.70
  80.7 0.4 copy.61
  81.1 3.8 %collective-permute-start.8 = (f32[1,375,256]{2,0,1:T(1,128)S(1)}, f32[1,375,256]{2,0,1:T(1,128)S(1)}, u32[]{:S(2)}, u32[]{:S(2)}) collective-permute-start(f32[1,375,256]{2,0,1:T(1,128)S(1)} %bitcast.158), channel_id=1, source_target_pairs={{0,4},{4,8},{8,12},{12,16},{16,20},{20,24},{24,28},{28,32},{32,36}... | collective-permute-start | bytes 1152008 | tf_op jit(solution)/shard_map/ppermute | solution.py:14
  84.9 4.6 %collective-permute-done.8 = f32[1,375,256]{2,0,1:T(1,128)S(1)} collective-permute-done((f32[1,375,256]{2,0,1:T(1,128)S(1)}, f32[1,375,256]{2,0,1:T(1,128)S(1)}, u32[]{:S(2)}, u32[]{:S(2)}) %collective-permute-start.8) | collective-permute-done | bytes 384032 | tf_op jit(solution)/shard_map/ppermute | solution.py:14
  89.5 0.5 fusion.36
  90.0 2.1 %collective-permute-start.9 = (f32[1,375,256]{2,0,1:T(1,128)S(1)}, f32[1,375,256]{2,0,1:T(1,128)S(1)}, u32[]{:S(2)}, u32[]{:S(2)}) collective-permute-start(f32[1,375,256]{2,0,1:T(1,128)S(1)} %fusion.36), channel_id=1, source_target_pairs={{4,0},{8,4},{12,8},{16,12},{20,16},{24,20},{28,24},{32,28},{36,32}... | collective-permute-start | bytes 1152008 | tf_op jit(solution)/shard_map/ppermute | solution.py:14
  92.2 7.6 %collective-permute-done.9 = f32[1,375,256]{2,0,1:T(1,128)S(1)} collective-permute-done((f32[1,375,256]{2,0,1:T(1,128)S(1)}, f32[1,375,256]{2,0,1:T(1,128)S(1)}, u32[]{:S(2)}, u32[]{:S(2)}) %collective-permute-start.9) | collective-permute-done | bytes 384032 | tf_op jit(solution)/shard_map/ppermute | solution.py:14
  99.8 0.5 fusion.35
  100.3 0.0 copy-start.5
  100.3 0.7 fusion.39
  101.0 0.8 copy.30
  101.8 0.0 all-gather.2.cloned.1.call-update
  101.8 0.0 copy-done.5
  101.8 0.1 reshape.96
  101.9 32.0 %all-gather.2.cloned.1.call-done = bf16[1,8,375,256]{3,2,0,1:T(8,128)(2,1)} async-done(((bf16[1,2,375,256]{3,2,0,1:T(8,128)(2,1)}), bf16[1,8,375,256]{3,2,0,1:T(8,128)(2,1)}) %all-gather.2.cloned.1.call-update) | async-done | bytes 1536016 | tf_op jit(solution)/shard_map/all_gather | solution.py:57
  133.9 0.0 copy-start.6
  133.9 5.0 %gather_fusion = bf16[32,375,256]{2,1,0:T(8,128)(2,1)} fusion(bf16[8,375,256]{2,1,0:T(8,128)(2,1)} %bitcast.154, s32[1024]{0:T(1024)S(1)} %pad_clamp_fusion), kind=kCustom, calls=%fused_computation | custom fusion | bytes 12288128 | tf_op jit(solution)/shard_map/jit(_take)/gather | solution.py:58
  138.9 0.0 copy-done.6
  138.9 11.0 %fusion.28 = f32[2,256,375]{1,2,0:T(8,128)S(1)} fusion(bf16[2,375,375]{2,0,1:T(2,128)(2,1)S(1)} %bitcast.160, bf16[2,16,375,375]{3,1,2,0:T(8,128)(2,1)} %bitcast.159, bf16[2,16,375,256]{3,2,1,0:T(8,128)(2,1)} %bitcast.155, pred[2,16]{1,0:T(4,128)(4,1)S(1)} %compare_and_fusion), kind=kOutput, calls=%fused_computation.41 | convolution fusion | flops 2451264000 | bytes 16474532 | tf_op jit(solution)/shard_map/jab,jbr->jar/dot_general | solution.py:60
  150.0 1.8 %fusion.27 = f32[1,2,375,256]{3,1,2,0:T(2,128)} fusion(f32[2,256,375]{1,2,0:T(8,128)S(1)} %fusion.28, pred[2]{0:T(512)(128)(4,1)S(1)} %get-tuple-element.6, f32[1,1,375,256]{3,1,2,0:T(1,128)S(1)} %fusion.35, f32[1,1,375,256]{3,1,2,0:T(1,128)S(1)} %bitcast.157), kind=kLoop, calls=%fused_computation.38 | loop fusion | flops 576000 | bytes 2304002 | tf_op jit(solution)/shard_map/broadcast_in_dim | solution.py:67
  (11 shorter events, 0.2 us)
Async XLA Ops:
  6.5 73.5 %copy-start = (bf16[1,2,375,375]{3,1,2,0:T(2,128)(2,1)S(1)}, bf16[1,2,375,375]{3,1,2,0:T(2,128)(2,1)}, u32[]{:S(2)}) copy-start(bf16[1,2,375,375]{3,1,2,0:T(2,128)(2,1)} %param.11) | copy-start | bytes 1687504
  6.5 127.4 %all-gather.2.cloned.1.call-start = ((), (), s32[]{:S(2)}) async-start(), calls=%async_computation | async-start | bytes 1925120 | tf_op jit(solution)/shard_map/all_gather | solution.py:57
  8.1 5.7 %collective-permute-start = (f32[192,256]{1,0:T(8,128)S(1)}, f32[192,256]{1,0:T(8,128)S(1)}, u32[]{:S(2)}, u32[]{:S(2)}) collective-permute-start(f32[192,256]{1,0:T(8,128)S(1)} %convolution_bitcast_fusion.14), channel_id=1, source_target_pairs={{0,1},{1,0},{2,3},{3,2},{4,5},{5,4},{6,7},{7,6},{8,9},{9,8},{10,11... | collective-permute-start | bytes 589832 | tf_op jit(solution)/shard_map/ppermute | solution.py:47
  13.8 7.1 %collective-permute-start.1 = (f32[192,256]{1,0:T(8,128)S(1)}, f32[192,256]{1,0:T(8,128)S(1)}, u32[]{:S(2)}, u32[]{:S(2)}) collective-permute-start(f32[192,256]{1,0:T(8,128)S(1)} %add.69), channel_id=1, source_target_pairs={{0,2},{1,3},{2,0},{3,1},{4,6},{5,7},{6,4},{7,5},{8,10},{9,11},{10,... | collective-permute-start | bytes 589832 | tf_op jit(solution)/shard_map/ppermute | solution.py:47
  22.4 4.6 %collective-permute-start.2 = (f32[192,256]{1,0:T(8,128)S(1)}, f32[192,256]{1,0:T(8,128)S(1)}, u32[]{:S(2)}, u32[]{:S(2)}) collective-permute-start(f32[192,256]{1,0:T(8,128)S(1)} %convolution_bitcast_fusion.13), channel_id=1, source_target_pairs={{0,4},{4,0},{8,12},{12,8},{16,20},{20,16},{24,28},{28,24},{32,36},... | collective-permute-start | bytes 589832 | tf_op jit(solution)/shard_map/ppermute | solution.py:8
  28.6 6.2 %collective-permute-start.3 = (f32[192,256]{1,0:T(8,128)S(1)}, f32[192,256]{1,0:T(8,128)S(1)}, u32[]{:S(2)}, u32[]{:S(2)}) collective-permute-start(f32[192,256]{1,0:T(8,128)S(1)} %convolution_bitcast_fusion.12), channel_id=1, source_target_pairs={{0,8},{4,12},{8,0},{12,4},{16,24},{20,28},{24,16},{28,20},{32,40},... | collective-permute-start | bytes 589832 | tf_op jit(solution)/shard_map/ppermute | solution.py:8
  36.3 11.4 %collective-permute-start.4 = (f32[192,256]{1,0:T(8,128)S(1)}, f32[192,256]{1,0:T(8,128)S(1)}, u32[]{:S(2)}, u32[]{:S(2)}) collective-permute-start(f32[192,256]{1,0:T(8,128)S(1)} %convolution_bitcast_fusion.11), channel_id=1, source_target_pairs={{0,16},{4,20},{8,24},{12,28},{16,0},{20,4},{24,8},{28,12},{32,48},... | collective-permute-start | bytes 589832 | tf_op jit(solution)/shard_map/ppermute | solution.py:8
  49.3 28.1 %copy-start.4 = (f32[192,192]{1,0:T(8,128)S(1)}, f32[192,192]{1,0:T(8,128)}, u32[]{:S(2)}) copy-start(f32[192,192]{1,0:T(8,128)} %param.15) | copy-start | bytes 442372
  49.3 13.8 %collective-permute-start.5 = (f32[192,256]{1,0:T(8,128)S(1)}, f32[192,256]{1,0:T(8,128)S(1)}, u32[]{:S(2)}, u32[]{:S(2)}) collective-permute-start(f32[192,256]{1,0:T(8,128)S(1)} %convolution_bitcast_fusion.10), channel_id=1, source_target_pairs={{0,32},{4,36},{8,40},{12,44},{16,48},{20,52},{24,56},{28,60},{32,0... | collective-permute-start | bytes 589832 | tf_op jit(solution)/shard_map/ppermute | solution.py:8
  63.1 14.6 %copy-start.1 = (f32[1,6,192,192]{3,2,1,0:T(8,128)S(1)}, f32[1,6,192,192]{3,2,1,0:T(8,128)}, u32[]{:S(2)}) copy-start(f32[1,6,192,192]{3,2,1,0:T(8,128)} %param.14) | copy-start | bytes 2654212
  64.7 5.0 %collective-permute-start.6 = (f32[192,256]{1,0:T(8,128)S(1)}, f32[192,256]{1,0:T(8,128)S(1)}, u32[]{:S(2)}, u32[]{:S(2)}) collective-permute-start(f32[192,256]{1,0:T(8,128)S(1)} %convolution_bitcast_fusion.9), channel_id=1, source_target_pairs={{0,64},{4,68},{8,72},{12,76},{16,80},{20,84},{24,88},{28,92},{32,9... | collective-permute-start | bytes 589832 | tf_op jit(solution)/shard_map/ppermute | solution.py:8
  71.2 6.1 %collective-permute-start.7 = (f32[192,256]{1,0:T(8,128)S(1)}, f32[192,256]{1,0:T(8,128)S(1)}, u32[]{:S(2)}, u32[]{:S(2)}) collective-permute-start(f32[192,256]{1,0:T(8,128)S(1)} %convolution_bitcast_fusion.8), channel_id=1, source_target_pairs={{0,128},{4,132},{8,136},{12,140},{16,144},{20,148},{24,152},{28,15... | collective-permute-start | bytes 589832 | tf_op jit(solution)/shard_map/ppermute | solution.py:8
  78.7 1.0 copy-start.3
  79.0 1.1 copy-start.2
  81.1 8.4 %collective-permute-start.8 = (f32[1,375,256]{2,0,1:T(1,128)S(1)}, f32[1,375,256]{2,0,1:T(1,128)S(1)}, u32[]{:S(2)}, u32[]{:S(2)}) collective-permute-start(f32[1,375,256]{2,0,1:T(1,128)S(1)} %bitcast.158), channel_id=1, source_target_pairs={{0,4},{4,8},{8,12},{12,16},{16,20},{20,24},{24,28},{28,32},{32,36}... | collective-permute-start | bytes 1152008 | tf_op jit(solution)/shard_map/ppermute | solution.py:14
  90.0 9.7 %collective-permute-start.9 = (f32[1,375,256]{2,0,1:T(1,128)S(1)}, f32[1,375,256]{2,0,1:T(1,128)S(1)}, u32[]{:S(2)}, u32[]{:S(2)}) collective-permute-start(f32[1,375,256]{2,0,1:T(1,128)S(1)} %fusion.36), channel_id=1, source_target_pairs={{4,0},{8,4},{12,8},{16,12},{20,16},{24,20},{28,24},{32,28},{36,32}... | collective-permute-start | bytes 1152008 | tf_op jit(solution)/shard_map/ppermute | solution.py:14
  100.3 1.5 copy-start.5
  133.9 5.0 %copy-start.6 = (bf16[1,2,375,375]{3,1,2,0:T(2,128)(2,1)S(1)}, bf16[1,2,375,375]{3,1,2,0:T(2,128)(2,1)}, u32[]{:S(2)}) copy-start(bf16[1,2,375,375]{3,1,2,0:T(2,128)(2,1)} %param.12) | copy-start | bytes 1687504
Sparse Core Ops, SparseCore 0:
  101.9 31.9 all-gather.1
